TPU v7x, 32 devices: a whole 2x2x4 slice. The times are simulated.
32 devices in a mesh: rows: 8 (over y, x, core), probe: 4 (over z).
Axes of the slice: x: 2, y: 2, z: 4, core: 2. Of those that a mesh axis runs over, the one named last changes fastest.
Arguments:
- points: float32 [64, 3, 128], P('rows'), may hold values from 0 to 1
- observations: float32 [64, 128], P('rows'), may hold values from -6 to 6
- probes: float32 [64, 64, 128], P('rows', 'probe'), may hold values from -150 to 150
- neighbours: int32 [64, 3], P('rows'), may hold values from 0 to 63, as said below
- block_position: int32 [64], P('rows'), may hold values from 0 to 63, as said below
Outputs:
- whitened: float32 [64, 128], P('rows')
- block_terms: float32 [64], P('rows')
- tridiagonal: float32 [64, 3], P('probe')
- remainder: float32 [64, 64, 128], P('rows', 'probe')
Inputs may be any that keep to these rules, and one draw needn't show every extreme that they name: block_position is a permutation of the block ids; the block with id i sits at position block_position[i], on index block_position[i] // 8 of rows. neighbours[b] lists three block ids, which may repeat and may name the block at b itself. Over the 24 references of the blocks of one index of rows, the positions of the named blocks fall at most 6 times on the blocks of any one index of rows, and exactly 6 times on those of some index, for every index.
All inputs are finite; a program needn't handle non-finite values.
Results may differ from a plain program's by a relative error of at most 0.0003.
Values sent between devices are 32-bit elements; how exact they have to be, the bound alone decides.
A program may use at most 64 MiB of HBM per device.

v0:
```python
import functools
import math

import jax
import jax.numpy as jnp
from jax import lax
from jax.experimental import pallas as pl
from jax.experimental.pallas import tpu as pltpu
from jax.sharding import PartitionSpec as P

length_scale = 0.3
nugget = 0.25
epsilon = 1e-06
highest = lax.Precision.HIGHEST
chunk = 8
width = 4


def dot(left, right):
    return jnp.dot(left, right, precision=highest, preferred_element_type=jnp.float32)


def dot_nt(left, right):
    return lax.dot_general(
        left, right, (((1,), (1,)), ((), ())), precision=highest,
        preferred_element_type=jnp.float32,
    )


def pivot_factor(rows, e):
    e = [list(r) for r in e]
    y = list(rows)
    inv = []
    product = None
    for k in range(width):
        d = e[k][k]
        s = lax.rsqrt(d)
        s = s * (1.5 - 0.5 * d * s * s)
        inv.append(s)
        product = s if product is None else product * s
        y[k] = y[k] * s
        for m in range(k + 1, width):
            e[m][k] = e[m][k] * s
        for m in range(k + 1, width):
            y[m] = y[m] - e[m][k] * y[k]
            for n in range(k + 1, m + 1):
                e[m][n] = e[m][n] - e[m][k] * e[n][k]
    r = list(y)
    for k in reversed(range(width)):
        for m in range(k + 1, width):
            r[k] = r[k] - e[m][k] * r[m]
        r[k] = r[k] * inv[k]
    return y, r, jnp.log(product)


def sweep(mats):
    count = len(mats[0])
    shape = mats[0][0].shape
    lane = lax.broadcasted_iota(jnp.int32, shape, 1)
    sub = lax.broadcasted_iota(jnp.int32, shape, 0)
    segment = max(1, count // 4)

    def full(x):
        return jnp.broadcast_to(x, shape)

    def step(start, t, carry):
        mats, logs = carry
        mats = [list(m) for m in mats]
        logs = list(logs)
        for o in range(0, chunk, width):
            picked = (lane >= o) & (lane < o + width)
            for b in range(len(mats)):
                chunks = mats[b]
                top = chunks[0]
                cols = [full(top[:, o + k : o + k + 1]) for k in range(width)]
                rows = [full(top[o + k : o + k + 1, :]) for k in range(width)]
                e = [[full(cols[k][o + m : o + m + 1, :]) for k in range(width)] for m in range(width)]
                rows = [
                    jnp.where(lane == o + k, 1.0, jnp.where(picked, 0.0, rows[k]))
                    for k in range(width)
                ]
                kept, r, term = pivot_factor(rows, e)
                logs[b] = logs[b] + term
                for p in range(count - start):
                    old = chunks[p]
                    if p == 0 and o + width == chunk:
                        new = old
                    else:
                        if p:
                            cols = [full(old[:, o + k : o + k + 1]) for k in range(width)]
                        new = jnp.where(picked, 0.0, old)
                        for k in range(width):
                            new = new - cols[k] * r[k]
                    if p == 0:
                        new = jnp.where(sub >= o + width, new, old)
                        for k in range(width):
                            new = jnp.where(sub == o + k, kept[k], new)
                    elif p > count - start - segment:
                        new = jnp.where(t + p < count, new, old)
                    chunks[p] = new
        turned = []
        for chunks in mats:
            chunks = [pltpu.roll(c, shape[1] - chunk, 1) for c in chunks]
            turned.append(tuple(chunks[1:] + chunks[:1]))
        return tuple(turned), tuple(logs)

    zero = jnp.zeros(shape, jnp.float32)
    carry = (mats, tuple(zero for _ in mats))
    for start in range(0, count, segment):
        carry = lax.fori_loop(start, start + segment, functools.partial(step, start), carry)
    return carry


MESH = pl.DeviceIdType.MESH


def to_peers(axis, count, source, target, send_sem, recv_sem):
    me = lax.axis_index(axis)
    copies = []
    for p in range(1, count):
        peer = lax.rem(me + p, count)
        copies.append(
            pltpu.make_async_remote_copy(
                src_ref=source(peer),
                dst_ref=target,
                send_sem=send_sem.at[p - 1],
                recv_sem=recv_sem.at[p - 1],
                device_id={axis: peer},
                device_id_type=MESH,
            )
        )
    for copy in copies:
        copy.start()
    return copies


def wait_all(copies):
    for copy in copies:
        copy.wait()


def greet(counts):
    barrier = pltpu.get_barrier_semaphore()
    total = 0
    for axis, count in counts:
        for p in range(1, count):
            peer = lax.rem(lax.axis_index(axis) + p, count)
            pl.semaphore_signal(barrier, inc=1, device_id={axis: peer}, device_id_type=MESH)
            total += 1
    pl.semaphore_wait(barrier, total)


def gather_kernel(count, *refs):
    half = 4
    sources, targets, (send_sem, recv_sem, own_sem) = refs[:half], refs[half : 2 * half], refs[2 * half :]
    me = lax.axis_index("rows")
    greet((("rows", count),))
    copies = []
    for i in range(half):
        copies += to_peers(
            "rows", count, lambda peer: sources[i], targets[i].at[me], send_sem.at[i], recv_sem.at[i]
        )
    owns = [
        pltpu.make_async_copy(sources[i], targets[i].at[me], own_sem.at[i]) for i in range(half)
    ]
    for own in owns:
        own.start()
    for own in owns:
        own.wait()
    wait_all(copies)


def gather_rows(count, arrays):
    vmem = pl.BlockSpec(memory_space=pltpu.VMEM)
    return pl.pallas_call(
        functools.partial(gather_kernel, count),
        out_shape=[jax.ShapeDtypeStruct((count,) + a.shape, a.dtype) for a in arrays],
        in_specs=[vmem] * len(arrays),
        out_specs=[vmem] * len(arrays),
        scratch_shapes=[
            pltpu.SemaphoreType.DMA((len(arrays), count - 1)),
            pltpu.SemaphoreType.DMA((len(arrays), count - 1)),
            pltpu.SemaphoreType.DMA((len(arrays),)),
        ],
        compiler_params=pltpu.CompilerParams(collective_id=0, has_side_effects=True),
    )(*arrays)


def plan_kernel(capacity, first_ref, near_ref, pos_ref, slot_ref, local_ref, seen_ref):
    count, blocks = near_ref.shape[:2]
    me = first_ref[0]

    def position(owner, b, j):
        ident = near_ref[owner, b, j]
        return pos_ref[ident // blocks, 0, ident % blocks]

    for i in range(count * capacity):
        slot_ref[i] = 3 * blocks
        local_ref[i] = -1
    for i in range(count):
        seen_ref[i] = 0

    def place_own(b, c):
        for j in range(3):
            row = position(me, b, j)
            at = row // blocks
            rank = seen_ref[at]
            seen_ref[at] = rank + 1
            slot_ref[at * capacity + rank] = b * 3 + j
            local_ref[at * capacity + rank] = row % blocks
        return c

    lax.fori_loop(0, blocks, place_own, 0)


def plan_slots(first, near, positions, capacity):
    count = near.shape[0]
    smem = pl.BlockSpec(memory_space=pltpu.SMEM)
    slots = jax.ShapeDtypeStruct((count * capacity,), jnp.int32)
    return pl.pallas_call(
        functools.partial(plan_kernel, capacity),
        out_shape=(slots, slots),
        in_specs=[smem] * 3,
        out_specs=(smem, smem),
        scratch_shapes=[pltpu.SMEM((count,), jnp.int32)],
    )(first, near, positions)


def build_kernels(near_rows, me, first, points_ref, a_ref):
    nb = a_ref.shape[0]
    blocks, _, bs = points_ref.shape[1:]

    def part(i):
        return slice(i * bs, (i + 1) * bs)

    same = lax.broadcasted_iota(jnp.int32, (bs, bs), 0) == lax.broadcasted_iota(
        jnp.int32, (bs, bs), 1
    )
    for b in range(nb):
        at = [(row // blocks, row % blocks) for row in near_rows[b]] + [(me, first + b)]
        rows = [points_ref[o, r] for o, r in at]
        pad = jnp.zeros((chunk - rows[0].shape[0], bs), jnp.float32)
        cols = [jnp.transpose(jnp.concatenate([row, pad], axis=0)) for row in rows]
        for i in range(4):
            for k in range(i + 1):
                dist_sq = None
                for c in range(3):
                    off = cols[i][:, c : c + 1] - rows[k][c : c + 1, :]
                    dist_sq = off * off if dist_sq is None else dist_sq + off * off
                value = 1.0 / (1.0 + dist_sq * (1.0 / (length_scale * length_scale)))
                if i == k:
                    value = value + jnp.where(same, nugget, 0.0)
                a_ref[b, part(i), part(k)] = value


def factor_blocks(near_rows, me, first, values_ref, a_ref, g_ref, wt_ref):
    nb, bs = g_ref.shape[:2]
    blocks = values_ref.shape[1]

    def part(i):
        return slice(i * bs, (i + 1) * bs)

    def load(j):
        return tuple(
            tuple(
                a_ref[b, j * bs + i * chunk : j * bs + (i + 1) * chunk, part(j)]
                for i in range(bs // chunk)
            )
            for b in range(nb)
        )

    below = lax.broadcasted_iota(jnp.int32, (bs, bs), 0) >= lax.broadcasted_iota(
        jnp.int32, (bs, bs), 1
    )
    invs = []
    for j in range(4):
        low, logs = sweep(load(j))
        invs.append([jnp.where(below, jnp.concatenate(low[b], axis=0), 0.0) for b in range(nb)])
        if j == 3:
            break
        for b in range(nb):
            scaled = dot_nt(a_ref[b, (j + 1) * bs :, part(j)], invs[j][b])
            for i in range(j + 1, 4):
                row = scaled[(i - j - 1) * bs : (i - j) * bs]
                a_ref[b, part(i), (j + 1) * bs : (i + 1) * bs] -= dot_nt(
                    row, scaled[: (i - j) * bs]
                )
            a_ref[b, (j + 1) * bs :, part(j)] = scaled
            a_ref[b, part(j), part(j)] = invs[j][b]
    for b in range(nb):
        low_inv = invs[3][b]
        x2 = dot(a_ref[b, part(3), part(2)], a_ref[b, part(2), part(2)])
        x1 = dot(
            a_ref[b, part(3), part(1)] - dot(x2, a_ref[b, part(2), part(1)]),
            a_ref[b, part(1), part(1)],
        )
        x0 = dot(
            a_ref[b, part(3), part(0)]
            - dot(x1, a_ref[b, part(1), part(0)])
            - dot(x2, a_ref[b, part(2), part(0)]),
            a_ref[b, part(0), part(0)],
        )
        g_ref[b, :, part(3)] = low_inv
        for i, x in enumerate((x0, x1, x2)):
            g_ref[b, :, part(i)] = -dot(low_inv, x)
        at = [(row // blocks, row % blocks) for row in near_rows[b]] + [(me, first + b)]
        values = jnp.concatenate(
            [jnp.broadcast_to(values_ref[o, pl.ds(r, 1)], (chunk, bs)) for o, r in at], axis=1
        )
        w = dot_nt(values, g_ref[b])
        square = jnp.sum(w[:1] * w[:1], axis=1, keepdims=True)
        term = (logs[b] - 0.5 * square) * (1.0 / bs) - 0.5 * math.log(2.0 * math.pi)
        wt_ref[b] = jnp.concatenate([w, term], axis=1)


def main_kernel(
    count, depth, capacity,
    near_ref, pos_ref, slot_ref, local_ref, points_ref, values_ref, probes_ref,
    rem_ref, tri_ref, w_ref, t_ref,
    a_ref, g_ref, wt_all, probes_all, q, z, sp,
    in1s, in1r, in2s, in2r, out1s, out1r, out2s, out2r, e1s, e1r, e2s, e2r,
    sb1, sb2, rb1, rb2, zsem, rsem, own_sem,
):
    me = lax.axis_index("rows")
    level = lax.axis_index("probe")
    blocks, cols, bs = probes_ref.shape
    total = blocks * count
    nb = g_ref.shape[0]
    cells = total * bs

    def position(b, j):
        ident = near_ref[me, b, j]
        return pos_ref[ident // blocks, 0, ident % blocks]

    def over_rows(i, source, target):
        return to_peers("rows", count, source, target, rsem.at[2 * i], rsem.at[2 * i + 1])

    def over_probe(i, source, target):
        return to_peers("probe", depth, source, target, zsem.at[2 * i], zsem.at[2 * i + 1])

    greet((("rows", count), ("probe", depth)))
    line = lax.broadcasted_iota(jnp.int32, (cols, bs), 0)
    here = pl.ds(me * blocks, blocks)
    probe_copies = over_rows(0, lambda peer: probes_ref, probes_all.at[here])
    keep = pltpu.make_async_copy(probes_ref, probes_all.at[here], own_sem)
    keep.start()

    first = level * nb
    near_rows = [[position(first + b, j) for j in range(3)] for b in range(nb)]
    build_kernels(near_rows, me, first, points_ref, a_ref)

    def inner(f):
        acc = jnp.zeros((cols, bs), jnp.float32)
        for c in range(total):
            acc = acc + f(c)
        return jnp.sum(acc, axis=1, keepdims=True)

    def send_in(i, source, s, r):
        for b in range(blocks):
            parts = [source[position(b, j)] for j in range(3)] + [source[me * blocks + b]]
            s[b // nb, b % nb] = jnp.concatenate(parts, axis=1)
        copies = over_probe(i, lambda peer: s.at[peer], r.at[level])
        r[level] = s[level]
        return copies

    keep.wait()
    wait_all(probe_copies)
    scale = 1.0 / jnp.sqrt(inner(lambda c: probes_all[c] * probes_all[c]) / cells + epsilon)
    for c in range(total):
        q[c] = probes_all[c] * scale
    in_copies = send_in(0, q, in1s, in1r)
    sp[3 * blocks] = jnp.zeros((cols, bs), jnp.float32)
    factor_blocks(near_rows, me, first, values_ref, a_ref, g_ref, wt_all.at[level])
    wt_copies = over_probe(1, lambda peer: wt_all.at[level], wt_all.at[level])

    def apply_operator(i, inr, outs, outr, es, er, sb, rb):
        energy = jnp.zeros((depth * cols, bs), jnp.float32)
        for b in range(nb):
            stacked = jnp.concatenate([inr[d, b] for d in range(depth)], axis=0)
            projected = dot_nt(stacked, g_ref[b])
            energy = energy + projected * projected
            spread = dot(projected, g_ref[b])
            for d in range(depth):
                outs[d, b] = spread[d * cols : (d + 1) * cols]
        for d in range(depth):
            es[d] = energy[d * cols : (d + 1) * cols]
        copies = over_probe(2 * i, lambda peer: outs.at[peer], outr.at[level])
        copies += over_probe(2 * i + 1, lambda peer: es.at[peer], er.at[level])
        outr[level] = outs[level]
        er[level] = es[level]
        wait_all(copies)
        energy = er[0]
        for d in range(1, depth):
            energy = energy + er[d]
        for b in range(blocks):
            for j in range(3):
                sp[b * 3 + j] = outr[b // nb, b % nb, :, j * bs : (j + 1) * bs]
        for d in range(count):
            for k in range(capacity):
                sb[d, k] = sp[slot_ref[d * capacity + k]]
            sb[d, capacity] = energy
            tile = jnp.full((cols, bs), -1, jnp.int32)
            for k in range(capacity):
                tile = jnp.where(line == k, local_ref[d * capacity + k], tile)
            sb[d, capacity + 1] = tile.astype(jnp.float32)
        copies = over_rows(i, lambda peer: sb.at[peer], rb.at[me])
        rb[me] = sb[me]
        wait_all(copies)
        sums = [outr[b // nb, b % nb, :, 3 * bs :] for b in range(blocks)]
        energy = jnp.zeros((cols, bs), jnp.float32)
        for d in range(count):
            tile = rb[d, capacity + 1]
            for k in range(capacity):
                value = rb[d, k]
                local = jnp.broadcast_to(tile[k : k + 1, :], (cols, bs))
                for b in range(blocks):
                    sums[b] = sums[b] + jnp.where(local == b, value, 0.0)
            energy = energy + rb[d, capacity]
        return sums, jnp.sum(energy, axis=1, keepdims=True) / cells

    wait_all(in_copies)
    image, alpha_one = apply_operator(1, in1r, out1s, out1r, e1s, e1r, sb1, rb1)
    for b in range(blocks):
        z[me * blocks + b] = image[b]
    wait_all(over_rows(2, lambda peer: z.at[here], z.at[here]))

    def residue(c):
        r = z[c] - alpha_one * q[c]
        return r * r

    beta_one = jnp.sqrt(inner(residue) / cells + epsilon)
    over = 1.0 / beta_one
    for b in range(blocks):
        rem_ref[b] = q[me * blocks + b]
    for c in range(total):
        q[c] = (z[c] - alpha_one * q[c]) * over
    wait_all(send_in(4, q, in2s, in2r))
    image, alpha_two = apply_operator(3, in2r, out2s, out2r, e2s, e2r, sb2, rb2)
    for b in range(blocks):
        rem_ref[b] = image[b] - alpha_two * q[me * blocks + b] - beta_one * rem_ref[b]
    lane = lax.broadcasted_iota(jnp.int32, (cols, bs), 1)
    tri_ref[...] = jnp.where(lane == 0, alpha_one, jnp.where(lane == 1, beta_one, alpha_two))
    wait_all(wt_copies)
    for b in range(blocks):
        w_ref[b : b + 1] = wt_all[b // nb, b % nb, :1, :bs]
        t_ref[b : b + 1] = wt_all[b // nb, b % nb, :1, bs:]


def main_call(count, depth, capacity, near, positions, slots, received, points, values, probes):
    blocks, cols, bs = probes.shape
    total = blocks * count
    nb = blocks // depth
    smem = pl.BlockSpec(memory_space=pltpu.SMEM)
    vmem = pl.BlockSpec(memory_space=pltpu.VMEM)
    f32 = jnp.float32
    dma = pltpu.SemaphoreType.DMA
    wide = pltpu.VMEM((depth, nb, cols, 4 * bs), f32)
    small = pltpu.VMEM((depth, cols, bs), f32)
    exchange = pltpu.VMEM((count, capacity + 2, cols, bs), f32)
    return pl.pallas_call(
        functools.partial(main_kernel, count, depth, capacity),
        out_shape=(
            jax.ShapeDtypeStruct((blocks, cols, bs), f32),
            jax.ShapeDtypeStruct((cols, bs), f32),
            jax.ShapeDtypeStruct((blocks, bs), f32),
            jax.ShapeDtypeStruct((blocks, bs), f32),
        ),
        in_specs=[smem] * 4 + [vmem] * 3,
        out_specs=(vmem,) * 4,
        scratch_shapes=[
            pltpu.VMEM((nb, 4 * bs, 4 * bs), f32),
            pltpu.VMEM((nb, bs, 4 * bs), f32),
            pltpu.VMEM((depth, nb, chunk, 2 * bs), f32),
            pltpu.VMEM((total, cols, bs), f32),
            pltpu.VMEM((total, cols, bs), f32),
            pltpu.VMEM((total, cols, bs), f32),
            pltpu.VMEM((3 * blocks + 1, cols, bs), f32),
        ]
        + [wide] * 8
        + [small] * 4
        + [exchange] * 4
        + [dma((16, depth - 1)), dma((8, count - 1)), dma],
        compiler_params=pltpu.CompilerParams(collective_id=1, has_side_effects=True),
    )(near, positions, slots, received, points, values, probes)


def body(points, observations, probes, neighbours, block_position):
    count = lax.axis_size("rows")
    depth = lax.axis_size("probe")
    blocks = points.shape[0]
    capacity = max(2, 6 * blocks // count)
    points_all, values_all, near_all, positions = gather_rows(
        count, (points, observations, neighbours, block_position.reshape(1, blocks))
    )
    first = lax.axis_index("rows").astype(jnp.int32).reshape(1)
    slots, received = plan_slots(first, near_all, positions, capacity)
    remainder, tri, whitened, terms = main_call(
        count, depth, capacity, near_all, positions, slots, received,
        points_all, values_all, probes,
    )
    return (whitened, terms[:, 0], tri[:, :3], remainder)


def solution(mesh):
    placed = (
        P("rows", None, None),
        P("rows", None),
        P("rows", "probe", None),
        P("rows", None),
        P("rows"),
    )
    return jax.shard_map(
        body,
        mesh=mesh,
        in_specs=placed,
        out_specs=(P("rows", None), P("rows"), P("probe", None), P("rows", "probe", None)),
        check_vma=False,
    )
```

profile of v0, /device:TPU:1, one launch (start us, length us, event | category | flops | bytes accessed | tf_op | source)
XLA Modules:
  0.0 122.2 jit_solution(11735310226802141087)
XLA Ops:
  0.6 0.0 copy-start
  0.6 1.3 %copy.13.refs_2_ = s32[8,3]{1,0:T(8,128)} copy(s32[8,3]{0,1:T(4,128)} %param.8) | data formatting | bytes 192 | tf_op args[3]
  2.0 0.0 copy-done
  2.0 0.6 copy.12.refs_0_
  2.6 8.8 %shard_map.84 = (f32[8,8,3,128]{3,2,1,0:T(4,128)}, f32[8,8,128]{2,1,0:T(8,128)}, s32[8,8,3]{2,1,0:T(8,128)}, s32[8,1,8]{2,1,0:T(1,128)}) custom-call(f32[8,3,128]{2,1,0:T(4,128)} %copy.12.refs_0_, f32[8,128]{1,0:T(8,128)} %refs_1_.1, s32[8,3]{1,0:T(8,128)} %copy.13.refs_2_, s32[1,8]{1,0:T(1,128)} %bitcast.4), custom_call_target="tpu_custom_call" | custom-call | tf_op jit(solution)/shard_map/pallas_call | solution.py:175
  11.4 2.3 %shard_map.85 = (s32[48]{0:T(128)}, s32[48]{0:T(128)}) custom-call(s32[1]{0:T(128)} %bitcast.1.first_ref, s32[8,8,3]{2,1,0:T(8,128)} %get-tuple-element.14.near_ref, s32[8,1,8]{2,1,0:T(1,128)} %get-tuple-element.15.pos_ref), custom_call_target="tpu_custom_call" | custom-call | tf_op jit(solution)/shard_map/pallas_call | solution.py:220
  13.7 104.5 %shard_map.86 = (f32[8,16,128]{2,1,0:T(8,128)}, f32[16,128]{1,0:T(8,128)}, f32[8,128]{1,0:T(8,128)}, f32[8,128]{1,0:T(8,128)}) custom-call(s32[8,8,3]{2,1,0:T(8,128)} %get-tuple-element.14.near_ref, s32[8,1,8]{2,1,0:T(1,128)} %get-tuple-element.15.pos_ref, s32[48]{0:T(128)} %get-tuple-element.16.slot_ref, s32[48]{0:T(128)} %get-tuple-element.17.local_ref, ...), custom_call_target="tpu_custom_call" | custom-call | tf_op jit(solution)/shard_map/pallas_call | solution.py:460
  118.2 0.0 copy-start.1
  118.2 1.3 %slice_reduce_fusion = f32[8]{0:T(128)} fusion(f32[8,128]{1,0:T(8,128)} %get-tuple-element.21), kind=kLoop, calls=%fused_computation | loop fusion | bytes 64 | tf_op jit(solution)/shard_map/slice | solution.py:501
  119.5 0.0 copy-done.1
  119.5 0.0 copy-start.2
  119.5 0.7 copy.14
  120.1 0.0 copy-done.2
  120.2 0.6 copy.17
  120.7 1.5 %copy.18 = f32[8,16,128]{2,1,0:T(8,128)} copy(f32[8,16,128]{2,1,0:T(8,128)} %get-tuple-element.39) | data formatting | bytes 131072
Async XLA Ops:
  0.6 1.4 %copy-start = (f32[8,3,128]{2,0,1:T(8,128)S(1)}, f32[8,3,128]{2,0,1:T(8,128)}, u32[]{:S(2)}) copy-start(f32[8,3,128]{2,0,1:T(8,128)} %param.5) | copy-start | bytes 36868
  118.2 1.3 %copy-start.1 = (f32[16,128]{1,0:T(8,128)S(1)}, f32[16,128]{1,0:T(8,128)}, u32[]{:S(2)}) copy-start(f32[16,128]{1,0:T(8,128)} %get-tuple-element.22) | copy-start | bytes 24580
  119.5 0.7 copy-start.2
where the time goes:
time: 123 us; the launch traced here: 122 us
  Pallas kernels  116 us (94%)
  local copies, waits for them, and re-layouts  6.01 us (5%)
    pallas_call x1, Pallas kernels, main_call(): pl.pallas_call(functools.partial(main_kernel, count, depth, capacity), ou...  104 us
    pallas_call x1, Pallas kernels, gather_rows(): pl.pallas_call(functools.partial(gather_kernel, count), out_shape=[jax.Sh...  8.8 us
    unnamed x11, local copies, waits for them, and re-layouts  4.7 us

commit v1 on v0

--- a/solution.py
+++ b/solution.py
@@ -13,7 +13,6 @@
 epsilon = 1e-06
 highest = lax.Precision.HIGHEST
 chunk = 8
-width = 4
 
 
 def dot(left, right):
@@ -27,30 +26,30 @@
     )
 
 
-def pivot_factor(rows, e):
-    e = [list(r) for r in e]
-    y = list(rows)
-    inv = []
-    product = None
+def invert_pivots(cols, units):
+    cols = list(cols)
+    width = len(cols)
+    low = list(units)
+    diag = None
     for k in range(width):
-        d = e[k][k]
-        s = lax.rsqrt(d)
-        s = s * (1.5 - 0.5 * d * s * s)
-        inv.append(s)
-        product = s if product is None else product * s
-        y[k] = y[k] * s
-        for m in range(k + 1, width):
-            e[m][k] = e[m][k] * s
-        for m in range(k + 1, width):
-            y[m] = y[m] - e[m][k] * y[k]
-            for n in range(k + 1, m + 1):
-                e[m][n] = e[m][n] - e[m][k] * e[n][k]
-    r = list(y)
-    for k in reversed(range(width)):
-        for m in range(k + 1, width):
-            r[k] = r[k] - e[m][k] * r[m]
-        r[k] = r[k] * inv[k]
-    return y, r, jnp.log(product)
+        at = units[k] > 0.5
+        for i in range(k):
+            low[i] = jnp.where(at, cols[i], low[i])
+        diag = cols[k] if diag is None else jnp.where(at, cols[k], diag)
+        pivot = jnp.broadcast_to(cols[k][k : k + 1, :], cols[k].shape)
+        scaled = (cols[k] - units[k]) * (1.0 / pivot)
+        for j in range(width):
+            if j != k:
+                cols[j] = cols[j] - scaled * jnp.broadcast_to(cols[j][k : k + 1, :], cols[j].shape)
+        cols[k] = units[k] - scaled
+    return cols, low, diag
+
+
+def weighted(parts, rows):
+    terms = [p * r for p, r in zip(parts, rows)]
+    while len(terms) > 1:
+        terms = [a + b for a, b in zip(terms[::2], terms[1::2])] + terms[len(terms) & ~1 :]
+    return terms[0]
 
 
 def sweep(mats):
@@ -58,57 +57,31 @@
     shape = mats[0][0].shape
     lane = lax.broadcasted_iota(jnp.int32, shape, 1)
     sub = lax.broadcasted_iota(jnp.int32, shape, 0)
-    segment = max(1, count // 4)
+    units = [jnp.where(sub == k, 1.0, 0.0) for k in range(chunk)]
 
     def full(x):
         return jnp.broadcast_to(x, shape)
 
-    def step(start, t, carry):
-        mats, logs = carry
-        mats = [list(m) for m in mats]
-        logs = list(logs)
-        for o in range(0, chunk, width):
-            picked = (lane >= o) & (lane < o + width)
-            for b in range(len(mats)):
-                chunks = mats[b]
-                top = chunks[0]
-                cols = [full(top[:, o + k : o + k + 1]) for k in range(width)]
-                rows = [full(top[o + k : o + k + 1, :]) for k in range(width)]
-                e = [[full(cols[k][o + m : o + m + 1, :]) for k in range(width)] for m in range(width)]
-                rows = [
-                    jnp.where(lane == o + k, 1.0, jnp.where(picked, 0.0, rows[k]))
-                    for k in range(width)
-                ]
-                kept, r, term = pivot_factor(rows, e)
-                logs[b] = logs[b] + term
-                for p in range(count - start):
-                    old = chunks[p]
-                    if p == 0 and o + width == chunk:
-                        new = old
-                    else:
-                        if p:
-                            cols = [full(old[:, o + k : o + k + 1]) for k in range(width)]
-                        new = jnp.where(picked, 0.0, old)
-                        for k in range(width):
-                            new = new - cols[k] * r[k]
-                    if p == 0:
-                        new = jnp.where(sub >= o + width, new, old)
-                        for k in range(width):
-                            new = jnp.where(sub == o + k, kept[k], new)
-                    elif p > count - start - segment:
-                        new = jnp.where(t + p < count, new, old)
-                    chunks[p] = new
-        turned = []
-        for chunks in mats:
-            chunks = [pltpu.roll(c, shape[1] - chunk, 1) for c in chunks]
-            turned.append(tuple(chunks[1:] + chunks[:1]))
-        return tuple(turned), tuple(logs)
-
-    zero = jnp.zeros(shape, jnp.float32)
-    carry = (mats, tuple(zero for _ in mats))
-    for start in range(0, count, segment):
-        carry = lax.fori_loop(start, start + segment, functools.partial(step, start), carry)
-    return carry
+    mats = [list(m) for m in mats]
+    logs = [jnp.zeros(shape, jnp.float32) for _ in mats]
+    for t in range(count):
+        o = t * chunk
+        picked = (lane >= o) & (lane < o + chunk)
+        unit = jnp.where(lane == sub + o, 1.0, 0.0)
+        for b, chunks in enumerate(mats):
+            top = chunks[t]
+            inv, low, diag = invert_pivots([full(top[:, o + k : o + k + 1]) for k in range(chunk)], units)
+            rows = jnp.where(picked, unit, top)
+            rows = [full(rows[k : k + 1, :]) for k in range(chunk)]
+            r = weighted(inv, rows)
+            chunks[t] = lax.rsqrt(diag) * weighted(low, rows)
+            logs[b] = logs[b] + jnp.log(diag)
+            r = [full(r[k : k + 1, :]) for k in range(chunk)]
+            for p in range(t + 1, count):
+                old = chunks[p]
+                cols = [full(old[:, o + k : o + k + 1]) for k in range(chunk)]
+                chunks[p] = jnp.where(picked, 0.0, old) - weighted(cols, r)
+    return mats, [-0.5 * jnp.sum(x[:, :1], axis=0, keepdims=True) for x in logs]
 
 
 MESH = pl.DeviceIdType.MESH
@@ -310,7 +283,7 @@
         w = dot_nt(values, g_ref[b])
         square = jnp.sum(w[:1] * w[:1], axis=1, keepdims=True)
         term = (logs[b] - 0.5 * square) * (1.0 / bs) - 0.5 * math.log(2.0 * math.pi)
-        wt_ref[b] = jnp.concatenate([w, term], axis=1)
+        wt_ref[b] = jnp.concatenate([w, jnp.broadcast_to(term, w.shape)], axis=1)
 
 
 def main_kernel(

time: 123 us -> 112 us (0.911)
  Pallas kernels: 116 us -> 105 us
    pallas_call x1, Pallas kernels: 104 us -> 93.7 us  [main_call(): pl.pallas_call(functools.partial(main_kernel, count, depth, capacity), ou...]
where the time goes in v1:
time: 112 us; the launch traced here: 111 us
  Pallas kernels  105 us (94%)
  local copies, waits for them, and re-layouts  6.01 us (5%)
    pallas_call x1, Pallas kernels, main_call(): pl.pallas_call(functools.partial(main_kernel, count, depth, capacity), ou...  93.7 us
    pallas_call x1, Pallas kernels, gather_rows(): pl.pallas_call(functools.partial(gather_kernel, count), out_shape=[jax.Sh...  8.8 us
    unnamed x11, local copies, waits for them, and re-layouts  4.7 us
    pallas_call x1, Pallas kernels, plan_slots(): pl.pallas_call(functools.partial(plan_kernel, capacity), out_shape=(slots...  2.27 us

profile of v1, /device:TPU:1, one launch (start us, length us, event | category | flops | bytes accessed | tf_op | source)
XLA Modules:
  0.0 111.5 jit_solution(8070099987496042770)
XLA Ops:
  0.6 0.0 copy-start
  0.6 1.3 %copy.13.refs_2_ = s32[8,3]{1,0:T(8,128)} copy(s32[8,3]{0,1:T(4,128)} %param.8) | data formatting | bytes 192 | tf_op args[3]
  2.0 0.0 copy-done
  2.0 0.6 copy.12.refs_0_
  2.6 8.8 %shard_map.84 = (f32[8,8,3,128]{3,2,1,0:T(4,128)}, f32[8,8,128]{2,1,0:T(8,128)}, s32[8,8,3]{2,1,0:T(8,128)}, s32[8,1,8]{2,1,0:T(1,128)}) custom-call(f32[8,3,128]{2,1,0:T(4,128)} %copy.12.refs_0_, f32[8,128]{1,0:T(8,128)} %refs_1_.1, s32[8,3]{1,0:T(8,128)} %copy.13.refs_2_, s32[1,8]{1,0:T(1,128)} %bitcast.4), custom_call_target="tpu_custom_call" | custom-call | tf_op jit(solution)/shard_map/pallas_call | solution.py:148
  11.4 2.3 %shard_map.85 = (s32[48]{0:T(128)}, s32[48]{0:T(128)}) custom-call(s32[1]{0:T(128)} %bitcast.1.first_ref, s32[8,8,3]{2,1,0:T(8,128)} %get-tuple-element.14.near_ref, s32[8,1,8]{2,1,0:T(1,128)} %get-tuple-element.15.pos_ref), custom_call_target="tpu_custom_call" | custom-call | tf_op jit(solution)/shard_map/pallas_call | solution.py:193
  13.7 93.7 %shard_map.86 = (f32[8,16,128]{2,1,0:T(8,128)}, f32[16,128]{1,0:T(8,128)}, f32[8,128]{1,0:T(8,128)}, f32[8,128]{1,0:T(8,128)}) custom-call(s32[8,8,3]{2,1,0:T(8,128)} %get-tuple-element.14.near_ref, s32[8,1,8]{2,1,0:T(1,128)} %get-tuple-element.15.pos_ref, s32[48]{0:T(128)} %get-tuple-element.16.slot_ref, s32[48]{0:T(128)} %get-tuple-element.17.local_ref, ...), custom_call_target="tpu_custom_call" | custom-call | tf_op jit(solution)/shard_map/pallas_call | solution.py:433
  107.4 0.0 copy-start.1
  107.4 1.3 %slice_reduce_fusion = f32[8]{0:T(128)} fusion(f32[8,128]{1,0:T(8,128)} %get-tuple-element.21), kind=kLoop, calls=%fused_computation | loop fusion | bytes 64 | tf_op jit(solution)/shard_map/slice | solution.py:474
  108.8 0.0 copy-done.1
  108.8 0.0 copy-start.2
  108.8 0.7 copy.14
  109.4 0.0 copy-done.2
  109.4 0.6 copy.17
  110.0 1.5 %copy.18 = f32[8,16,128]{2,1,0:T(8,128)} copy(f32[8,16,128]{2,1,0:T(8,128)} %get-tuple-element.39) | data formatting | bytes 131072
Async XLA Ops:
  0.6 1.4 %copy-start = (f32[8,3,128]{2,0,1:T(8,128)S(1)}, f32[8,3,128]{2,0,1:T(8,128)}, u32[]{:S(2)}) copy-start(f32[8,3,128]{2,0,1:T(8,128)} %param.5) | copy-start | bytes 36868
  107.4 1.3 %copy-start.1 = (f32[16,128]{1,0:T(8,128)S(1)}, f32[16,128]{1,0:T(8,128)}, u32[]{:S(2)}) copy-start(f32[16,128]{1,0:T(8,128)} %get-tuple-element.22) | copy-start | bytes 24580
  108.8 0.7 copy-start.2

commit v2 on v1

v2 whole, which is shorter than its diff:
```python
import functools
import math

import jax
import jax.numpy as jnp
from jax import lax
from jax.experimental import pallas as pl
from jax.experimental.pallas import tpu as pltpu
from jax.sharding import PartitionSpec as P

length_scale = 0.3
nugget = 0.25
epsilon = 1e-06
highest = lax.Precision.HIGHEST
chunk = 8


def dot(left, right):
    return jnp.dot(left, right, precision=highest, preferred_element_type=jnp.float32)


def dot_nt(left, right):
    return lax.dot_general(
        left, right, (((1,), (1,)), ((), ())), precision=highest,
        preferred_element_type=jnp.float32,
    )


def invert_pivots(cols, units):
    cols = list(cols)
    width = len(cols)
    low = list(units)
    diag = None

    def row(x, k):
        return jnp.broadcast_to(x[k : k + 1, :], x.shape)

    for k in range(0, width, 2):
        n = k + 1
        here, after = units[k] > 0.5, units[n] > 0.5
        a, b, c = row(cols[k], k), row(cols[n], k), row(cols[n], n)
        det = a * c - b * b
        over = 1.0 / det
        ratio = b * (1.0 / a)
        left, right = cols[k] - units[k], cols[n] - units[n]
        first = left * (c * over) - right * (b * over)
        second = right * (a * over) - left * (b * over)
        last = det * (1.0 / a)
        diag = a if diag is None else jnp.where(here, a, diag)
        diag = jnp.where(after, last, diag)
        for j in range(width):
            if j != k and j != n:
                upper, lower = row(cols[j], k), row(cols[j], n)
                if j < k:
                    low[j] = jnp.where(here, upper, low[j])
                    low[j] = jnp.where(after, lower - ratio * upper, low[j])
                cols[j] = cols[j] - (first * upper + second * lower)
        low[k] = jnp.where(after, -ratio, low[k])
        cols[k] = units[k] - first
        cols[n] = units[n] - second
        yield cols, low, diag


def weighted(parts, rows):
    terms = [p * r for p, r in zip(parts, rows)]
    while len(terms) > 1:
        terms = [a + b for a, b in zip(terms[::2], terms[1::2])] + terms[len(terms) & ~1 :]
    return terms[0]


def sweep(mats):
    pairs = [(mats[i], mats[min(i + 1, len(mats) - 1)]) for i in range(0, len(mats), 2)]
    count = len(mats[0])
    shape = mats[0][0].shape
    half = shape[1] // 2
    lane = lax.broadcasted_iota(jnp.int32, shape, 1)
    sub = lax.broadcasted_iota(jnp.int32, shape, 0)
    left = lane < half
    place = jnp.where(left, lane, lane - half)
    units = [jnp.where(sub == k, 1.0, 0.0) for k in range(chunk)]

    def full(x):
        return jnp.broadcast_to(x, shape)

    def swap(x):
        return pltpu.roll(x, half, 1)

    def pick(x, at):
        return jnp.where(left, full(x[:, at : at + 1]), full(x[:, half + at : half + at + 1]))

    packed = [
        [
            [jnp.where(left, x, swap(y)) for x, y in zip(one, two)],
            [jnp.where(left, swap(x), y) for x, y in zip(one, two)],
        ]
        for one, two in pairs
    ]
    logs = [jnp.zeros(shape, jnp.float32) for _ in pairs]
    waiting = []
    for t in range(count):
        side, o = divmod(t * chunk, half)
        picked = (place >= o) & (place < o + chunk)
        unit = jnp.where(place == sub + o, 1.0, 0.0)
        steps = [
            invert_pivots([pick(sides[side][t], o + k) for k in range(chunk)], units)
            for sides in packed
        ]
        found = None
        for k in range(0, chunk, 2):
            found = [next(step) for step in steps]
            share = -(-len(waiting) * 2 // (chunk - k))
            for update in waiting[:share]:
                update()
            waiting = waiting[share:]
        later = []
        for n, (sides, (inv, low, diag)) in enumerate(zip(packed, found)):
            scale = lax.rsqrt(diag)
            logs[n] = logs[n] + jnp.log(diag)
            r = []
            for s in range(2):
                rows = jnp.where(picked, unit, sides[s][t]) if s == side else sides[s][t]
                rows = [full(rows[k : k + 1, :]) for k in range(chunk)]
                move = weighted(inv, rows)
                sides[s][t] = scale * weighted(low, rows)
                r.append([full(move[k : k + 1, :]) for k in range(chunk)])

            def update(p, sides=sides, r=r, side=side, o=o, picked=picked):
                cols = [pick(sides[side][p], o + k) for k in range(chunk)]
                for s in range(2):
                    old = jnp.where(picked, 0.0, sides[s][p]) if s == side else sides[s][p]
                    sides[s][p] = old - weighted(cols, r[s])

            if t + 1 < count:
                update(t + 1)
            later.append([functools.partial(update, p) for p in range(t + 2, count)])
        waiting = [u for group in zip(*later) for u in group]
    out, sums = [], []
    for sides, total in zip(packed, logs):
        out.append([jnp.where(left, x, swap(y)) for x, y in zip(*sides)])
        out.append([jnp.where(left, swap(x), y) for x, y in zip(*sides)])
        total = -0.5 * jnp.sum(total, axis=0, keepdims=True)
        sums += [total[:, :1], total[:, half : half + 1]]
    return out[: len(mats)], sums[: len(mats)]


MESH = pl.DeviceIdType.MESH


def to_peers(axis, count, source, target, send_sem, recv_sem):
    me = lax.axis_index(axis)
    copies = []
    for p in range(1, count):
        peer = lax.rem(me + p, count)
        copies.append(
            pltpu.make_async_remote_copy(
                src_ref=source(peer),
                dst_ref=target,
                send_sem=send_sem.at[p - 1],
                recv_sem=recv_sem.at[p - 1],
                device_id={axis: peer},
                device_id_type=MESH,
            )
        )
    for copy in copies:
        copy.start()
    return copies


def wait_all(copies):
    for copy in copies:
        copy.wait()


def greet(counts):
    barrier = pltpu.get_barrier_semaphore()
    total = 0
    for axis, count in counts:
        for p in range(1, count):
            peer = lax.rem(lax.axis_index(axis) + p, count)
            pl.semaphore_signal(barrier, inc=1, device_id={axis: peer}, device_id_type=MESH)
            total += 1
    pl.semaphore_wait(barrier, total)


def gather_kernel(count, *refs):
    half = 4
    sources, targets, (send_sem, recv_sem, own_sem) = refs[:half], refs[half : 2 * half], refs[2 * half :]
    me = lax.axis_index("rows")
    greet((("rows", count),))
    copies = []
    for i in range(half):
        copies += to_peers(
            "rows", count, lambda peer: sources[i], targets[i].at[me], send_sem.at[i], recv_sem.at[i]
        )
    owns = [
        pltpu.make_async_copy(sources[i], targets[i].at[me], own_sem.at[i]) for i in range(half)
    ]
    for own in owns:
        own.start()
    for own in owns:
        own.wait()
    wait_all(copies)


def gather_rows(count, arrays):
    vmem = pl.BlockSpec(memory_space=pltpu.VMEM)
    return pl.pallas_call(
        functools.partial(gather_kernel, count),
        out_shape=[jax.ShapeDtypeStruct((count,) + a.shape, a.dtype) for a in arrays],
        in_specs=[vmem] * len(arrays),
        out_specs=[vmem] * len(arrays),
        scratch_shapes=[
            pltpu.SemaphoreType.DMA((len(arrays), count - 1)),
            pltpu.SemaphoreType.DMA((len(arrays), count - 1)),
            pltpu.SemaphoreType.DMA((len(arrays),)),
        ],
        compiler_params=pltpu.CompilerParams(collective_id=0, has_side_effects=True),
    )(*arrays)


def plan_kernel(capacity, depth, first_ref, near_ref, pos_ref, slot_ref, local_ref, seen_ref):
    count, blocks = near_ref.shape[0], near_ref.shape[2]
    me = first_ref[0]

    def position(owner, b, j):
        ident = near_ref[owner, j, b]
        return pos_ref[ident // blocks, 0, ident % blocks]

    nb = blocks // depth
    tiles = 4 * nb + 1
    for i in range(count * capacity):
        slot_ref[i] = depth * tiles
        local_ref[i] = -1
    for i in range(count):
        seen_ref[i] = 0

    def place_own(b, c):
        for j in range(3):
            row = position(me, b, j)
            at = row // blocks
            rank = seen_ref[at]
            seen_ref[at] = rank + 1
            slot_ref[at * capacity + rank] = b // nb * tiles + b % nb * 4 + j
            local_ref[at * capacity + rank] = row % blocks
        return c

    lax.fori_loop(0, blocks, place_own, 0)


def plan_slots(first, near, positions, capacity, depth):
    count = near.shape[0]
    smem = pl.BlockSpec(memory_space=pltpu.SMEM)
    slots = jax.ShapeDtypeStruct((count * capacity,), jnp.int32)
    return pl.pallas_call(
        functools.partial(plan_kernel, capacity, depth),
        out_shape=(slots, slots),
        in_specs=[smem] * 3,
        out_specs=(smem, smem),
        scratch_shapes=[pltpu.SMEM((count,), jnp.int32)],
    )(first, near, positions)


def build_kernels(near_rows, me, first, points_ref, a_ref):
    nb = a_ref.shape[0]
    _, blocks, bs = points_ref.shape[1:]

    def part(i):
        return slice(i * bs, (i + 1) * bs)

    same = lax.broadcasted_iota(jnp.int32, (bs, bs), 0) == lax.broadcasted_iota(
        jnp.int32, (bs, bs), 1
    )
    for b in range(nb):
        at = [(row // blocks, row % blocks) for row in near_rows[b]] + [(me, first + b)]
        rows = [[points_ref[o, c, pl.ds(r, 1), :] for c in range(3)] for o, r in at]
        pad = jnp.zeros((chunk - 3, bs), jnp.float32)
        cols = [jnp.transpose(jnp.concatenate(row + [pad], axis=0)) for row in rows]
        for i in range(4):
            for k in range(i + 1):
                dist_sq = None
                for c in range(3):
                    off = cols[i][:, c : c + 1] - rows[k][c]
                    dist_sq = off * off if dist_sq is None else dist_sq + off * off
                value = 1.0 / (1.0 + dist_sq * (1.0 / (length_scale * length_scale)))
                if i == k:
                    value = value + jnp.where(same, nugget, 0.0)
                a_ref[b, part(i), part(k)] = value


def factor_blocks(near_rows, me, first, values_ref, a_ref, g_ref, wt_ref, midway):
    nb, bs = g_ref.shape[:2]
    blocks = values_ref.shape[1]

    def part(i):
        return slice(i * bs, (i + 1) * bs)

    def load(j):
        return tuple(
            tuple(
                a_ref[b, j * bs + i * chunk : j * bs + (i + 1) * chunk, part(j)]
                for i in range(bs // chunk)
            )
            for b in range(nb)
        )

    below = lax.broadcasted_iota(jnp.int32, (bs, bs), 0) >= lax.broadcasted_iota(
        jnp.int32, (bs, bs), 1
    )
    invs = []
    for j in range(4):
        low, logs = sweep(load(j))
        invs.append([jnp.where(below, jnp.concatenate(low[b], axis=0), 0.0) for b in range(nb)])
        if j == 3:
            break
        if j == 0:
            midway()
        for b in range(nb):
            scaled = dot_nt(a_ref[b, (j + 1) * bs :, part(j)], invs[j][b])
            for i in range(j + 1, 4):
                row = scaled[(i - j - 1) * bs : (i - j) * bs]
                a_ref[b, part(i), (j + 1) * bs : (i + 1) * bs] -= dot_nt(
                    row, scaled[: (i - j) * bs]
                )
            a_ref[b, (j + 1) * bs :, part(j)] = scaled
            a_ref[b, part(j), part(j)] = invs[j][b]
    for b in range(nb):
        low_inv = invs[3][b]
        x2 = dot(a_ref[b, part(3), part(2)], a_ref[b, part(2), part(2)])
        x1 = dot(
            a_ref[b, part(3), part(1)] - dot(x2, a_ref[b, part(2), part(1)]),
            a_ref[b, part(1), part(1)],
        )
        x0 = dot(
            a_ref[b, part(3), part(0)]
            - dot(x1, a_ref[b, part(1), part(0)])
            - dot(x2, a_ref[b, part(2), part(0)]),
            a_ref[b, part(0), part(0)],
        )
        g_ref[b, :, part(3)] = low_inv
        for i, x in enumerate((x0, x1, x2)):
            g_ref[b, :, part(i)] = -dot(low_inv, x)
        at = [(row // blocks, row % blocks) for row in near_rows[b]] + [(me, first + b)]
        values = jnp.concatenate(
            [jnp.broadcast_to(values_ref[o, pl.ds(r, 1)], (chunk, bs)) for o, r in at], axis=1
        )
        w = dot_nt(values, g_ref[b])
        square = jnp.sum(w[:1] * w[:1], axis=1, keepdims=True)
        term = (logs[b] - 0.5 * square) * (1.0 / bs) - 0.5 * math.log(2.0 * math.pi)
        wt_ref[b] = jnp.concatenate([w, jnp.broadcast_to(term, w.shape)], axis=1)


def main_kernel(
    count, depth, capacity,
    near_ref, pos_ref, slot_ref, local_ref, points_ref, values_ref, probes_ref,
    rem_ref, tri_ref, w_ref, t_ref,
    a_ref, g_ref, wt_all, probes_all, q, q2, z, lts, ltr,
    ins, inr, outs, outr, sbs, rbs, zsem, rsem, own_sem,
):
    me = lax.axis_index("rows")
    level = lax.axis_index("probe")
    blocks, cols, bs = probes_ref.shape
    parts = len(z)
    span = cols // parts
    total = blocks * count
    nb = g_ref.shape[0]
    cells = total * bs

    def position(b, j):
        ident = near_ref[me, j, b]
        return pos_ref[ident // blocks, 0, ident % blocks]

    def over_rows(i, source, target):
        return to_peers("rows", count, source, target, rsem.at[2 * i], rsem.at[2 * i + 1])

    def over_probe(i, source, target):
        return to_peers("probe", depth, source, target, zsem.at[2 * i], zsem.at[2 * i + 1])

    greet((("rows", count), ("probe", depth)))
    here = pl.ds(me * blocks, blocks)
    probe_copies = over_rows(0, lambda peer: probes_ref, probes_all.at[here])
    keep = pltpu.make_async_copy(probes_ref, probes_all.at[here], own_sem)
    keep.start()

    first = level * nb
    near_rows = [[position(first + b, j) for j in range(3)] for b in range(nb)]
    build_kernels(near_rows, me, first, points_ref, a_ref)

    def inner(f):
        acc = [jnp.zeros((span, bs), jnp.float32) for _ in range(4)]
        for c in range(total):
            acc[c % 4] = acc[c % 4] + f(c)
        acc = (acc[0] + acc[1]) + (acc[2] + acc[3])
        return jnp.sum(acc, axis=1, keepdims=True)

    def rows_of(h):
        return slice(h * span, (h + 1) * span)

    def send_in(i, h, source):
        s, r = ins[i][h], inr[i][h]
        for b in range(blocks):
            at = [position(b, j) for j in range(3)] + [me * blocks + b]
            for j in range(4):
                s[b // nb, b % nb * 4 + j] = source[at[j]]
        copies = over_probe(1 + i * parts + h, lambda peer: s.at[peer], r.at[level])
        r[level] = s[level]
        return copies

    early = []

    def midway():
        keep.wait()
        wait_all(probe_copies)
        for h in range(parts):
            def part_of(c):
                return probes_all[c, rows_of(h), :]

            scale = 1.0 / jnp.sqrt(inner(lambda c: part_of(c) * part_of(c)) / cells + epsilon)
            for c in range(total):
                q[h][c] = part_of(c) * scale
            early.append(send_in(0, h, q[h]))
        line = lax.broadcasted_iota(jnp.int32, lts.shape[1:], 0)
        for d in range(count):
            tile = jnp.full(lts.shape[1:], -1, jnp.int32)
            for k in range(capacity):
                tile = jnp.where(line == k, local_ref[d * capacity + k], tile)
            lts[d] = tile.astype(jnp.float32)
        early.append(over_rows(1, lambda peer: lts.at[peer], ltr.at[me]))
        ltr[me] = lts[me]
        for i in range(2):
            for h in range(parts):
                outr[i][h][depth * (4 * nb + 1)] = jnp.zeros((span, bs), jnp.float32)

    factor_blocks(near_rows, me, first, values_ref, a_ref, g_ref, wt_all.at[level], midway)
    wt_copies = over_probe(0, lambda peer: wt_all.at[level], wt_all.at[level])
    tiles = 4 * nb + 1

    def multiply(i, h):
        source, s, r = inr[i][h], outs[i][h], outr[i][h]
        energy = jnp.zeros((depth * span, bs), jnp.float32)
        for b in range(nb):
            stacked = jnp.concatenate(
                [
                    jnp.concatenate([source[d, b * 4 + j] for j in range(4)], axis=1)
                    for d in range(depth)
                ],
                axis=0,
            )
            projected = dot_nt(stacked, g_ref[b])
            energy = energy + projected * projected
            spread = dot(projected, g_ref[b])
            for d in range(depth):
                for j in range(4):
                    s[d, b * 4 + j] = spread[d * span : (d + 1) * span, j * bs : (j + 1) * bs]
        for d in range(depth):
            s[d, 4 * nb] = energy[d * span : (d + 1) * span]
        copies = over_probe(
            1 + (2 + i) * parts + h, lambda peer: s.at[peer], r.at[pl.ds(level * tiles, tiles)]
        )
        r[pl.ds(level * tiles, tiles)] = s[level]
        return copies

    def transpose_out(i, h):
        source, s, r = outr[i][h], sbs[i][h], rbs[i][h]
        energy = source[4 * nb]
        for d in range(1, depth):
            energy = energy + source[d * tiles + 4 * nb]
        for d in range(count):
            for k in range(capacity):
                s[d, k] = source[slot_ref[d * capacity + k]]
            s[d, capacity] = energy
        copies = over_rows(2 + i * parts + h, lambda peer: s.at[peer], r.at[me])
        r[me] = s[me]
        return copies

    def collect(i, h):
        source, r = outr[i][h], rbs[i][h]
        sums = [source[b // nb * tiles + b % nb * 4 + 3] for b in range(blocks)]
        energy = jnp.zeros((span, bs), jnp.float32)
        for d in range(count):
            tile = ltr[d]
            for k in range(capacity):
                value = r[d, k]
                local = jnp.broadcast_to(tile[k : k + 1, :], (span, bs))
                for b in range(blocks):
                    sums[b] = sums[b] + jnp.where(local == b, value, 0.0)
            energy = energy + r[d, capacity]
        return sums, jnp.sum(energy, axis=1, keepdims=True) / cells

    def share(h):
        image, alpha = collect(0, h)
        for b in range(blocks):
            z[h][me * blocks + b] = image[b]
        return alpha, over_rows(2 + 2 * parts + h, lambda peer: z[h].at[here], z[h].at[here])

    def second(h, alpha):
        def residue(c):
            r = z[h][c] - alpha * q[h][c]
            return r * r

        beta = jnp.sqrt(inner(residue) / cells + epsilon)
        over = 1.0 / beta
        for c in range(total):
            q2[h][c] = (z[h][c] - alpha * q[h][c]) * over
        return beta, send_in(1, h, q2[h])

    every = range(parts)
    flying = []
    for h in every:
        wait_all(early[h])
        flying.append(multiply(0, h))
    for h in every:
        wait_all(flying[h])
        flying[h] = transpose_out(0, h)
    wait_all(early[parts])
    alpha_one, beta_one, alpha_two = {}, {}, {}
    for h in every:
        wait_all(flying[h])
        alpha_one[h], flying[h] = share(h)
    for h in every:
        wait_all(flying[h])
        beta_one[h], flying[h] = second(h, alpha_one[h])
    for h in every:
        wait_all(flying[h])
        flying[h] = multiply(1, h)
    for h in every:
        wait_all(flying[h])
        flying[h] = transpose_out(1, h)
    wait_all(wt_copies)
    for b in range(blocks):
        w_ref[b : b + 1] = wt_all[b // nb, b % nb, :1, :bs]
    terms = jnp.concatenate([wt_all[b // nb, b % nb, :1, bs:] for b in range(blocks)], axis=0)
    t_ref[...] = jnp.transpose(terms)[:1, :]
    for h in every:
        wait_all(flying[h])
        image, alpha_two[h] = collect(1, h)
        for b in range(blocks):
            rem_ref[b, rows_of(h), :] = (
                image[b] - alpha_two[h] * q2[h][me * blocks + b]
                - beta_one[h] * q[h][me * blocks + b]
            )
    lane = lax.broadcasted_iota(jnp.int32, (cols, bs), 1)

    def joined(x):
        return jnp.concatenate([x[h] for h in every], axis=0)

    tri = jnp.where(
        lane == 0, joined(alpha_one), jnp.where(lane == 1, joined(beta_one), joined(alpha_two))
    )
    tri_ref[...] = jnp.transpose(tri)[:3, :]


def main_call(count, depth, capacity, near, positions, slots, received, points, values, probes):
    blocks, cols, bs = probes.shape
    total = blocks * count
    nb = blocks // depth
    parts = max(1, cols // chunk)
    span = cols // parts
    smem = pl.BlockSpec(memory_space=pltpu.SMEM)
    vmem = pl.BlockSpec(memory_space=pltpu.VMEM)
    f32 = jnp.float32
    dma = pltpu.SemaphoreType.DMA

    def each(*shape):
        return [pltpu.VMEM(shape, f32) for _ in range(parts)]

    def both(*shape):
        return [each(*shape), each(*shape)]

    return pl.pallas_call(
        functools.partial(main_kernel, count, depth, capacity),
        out_shape=(
            jax.ShapeDtypeStruct((blocks, cols, bs), f32),
            jax.ShapeDtypeStruct((3, cols), f32),
            jax.ShapeDtypeStruct((blocks, bs), f32),
            jax.ShapeDtypeStruct((1, blocks), f32),
        ),
        in_specs=[smem] * 4 + [vmem] * 3,
        out_specs=(vmem,) * 4,
        scratch_shapes=[
            pltpu.VMEM((nb, 4 * bs, 4 * bs), f32),
            pltpu.VMEM((nb, bs, 4 * bs), f32),
            pltpu.VMEM((depth, nb, chunk, 2 * bs), f32),
            pltpu.VMEM((total, cols, bs), f32),
            each(total, span, bs),
            each(total, span, bs),
            each(total, span, bs),
            pltpu.VMEM((count, chunk, bs), f32),
            pltpu.VMEM((count, chunk, bs), f32),
            both(depth, nb * 4, span, bs),
            both(depth, nb * 4, span, bs),
            both(depth, nb * 4 + 1, span, bs),
            both(depth * (nb * 4 + 1) + 1, span, bs),
            both(count, capacity + 1, span, bs),
            both(count, capacity + 1, span, bs),
            dma((2 * (4 * parts + 1), depth - 1)),
            dma((2 * (3 * parts + 2), count - 1)),
            dma,
        ],
        compiler_params=pltpu.CompilerParams(collective_id=1, has_side_effects=True),
    )(near, positions, slots, received, points, values, probes)


def hand_kernel(*refs):
    half = len(refs) // 2
    for source, target in zip(refs[:half], refs[half:]):
        target[...] = source[...]


def hand_over(arrays):
    vmem = pl.BlockSpec(memory_space=pltpu.VMEM)
    return pl.pallas_call(
        hand_kernel,
        out_shape=[jax.ShapeDtypeStruct(a.shape, a.dtype) for a in arrays],
        in_specs=[vmem] * len(arrays),
        out_specs=[vmem] * len(arrays),
    )(*arrays)


def body(points, observations, probes, neighbours, block_position):
    count = lax.axis_size("rows")
    depth = lax.axis_size("probe")
    blocks = points.shape[0]
    capacity = max(2, 6 * blocks // count)
    points_all, values_all, near_all, positions = gather_rows(
        count,
        (
            jnp.transpose(points, (1, 0, 2)), observations, neighbours.T,
            block_position.reshape(1, blocks),
        ),
    )
    first = lax.axis_index("rows").astype(jnp.int32).reshape(1)
    slots, received = plan_slots(first, near_all, positions, capacity, depth)
    remainder, tri, whitened, terms = main_call(
        count, depth, capacity, near_all, positions, slots, received,
        points_all, values_all, probes,
    )
    remainder, tri, whitened, terms = hand_over((remainder, tri, whitened, terms))
    return (whitened, terms.reshape(blocks), tri.T, remainder)


def solution(mesh):
    placed = (
        P("rows", None, None),
        P("rows", None),
        P("rows", "probe", None),
        P("rows", None),
        P("rows"),
    )
    return jax.shard_map(
        body,
        mesh=mesh,
        in_specs=placed,
        out_specs=(P("rows", None), P("rows"), P("probe", None), P("rows", "probe", None)),
        check_vma=False,
    )
```

time: 112 us -> 84.6 us (0.76)
  Pallas kernels: 105 us -> 83.3 us
  local copies, waits for them, and re-layouts: 6.01 us -> 0 us
    pallas_call x1, Pallas kernels: 93.7 us -> 71.1 us  [main_call(): pl.pallas_call(functools.partial(main_kernel, count, depth, capacity), ou...]
    unnamed x11 -> x0, local copies, waits for them, and re-layouts: 4.7 us -> none
    slice x1 -> x0, local copies, waits for them, and re-layouts: 1.31 us -> none  [body(): return (whitened, terms[:, 0], tri[:, :3], remainder)]
    pallas_call x1 -> x2, Pallas kernels: 2.27 us -> 3.56 us  [the longest x1 2.07 us: plan_slots(): pl.pallas_call(functools.partial(plan_kernel, capacity, depth), out_shape...]
where the time goes in v2:
time: 84.6 us; the launch traced here: 83.9 us
  Pallas kernels  83.3 us (98%)
    pallas_call x1, Pallas kernels, main_call(): pl.pallas_call(functools.partial(main_kernel, count, depth, capacity), ou...  71.1 us
    pallas_call x1, Pallas kernels, gather_rows(): pl.pallas_call(functools.partial(gather_kernel, count), out_shape=[jax.Sh...  8.59 us
    pallas_call x1, Pallas kernels, plan_slots(): pl.pallas_call(functools.partial(plan_kernel, capacity, depth), out_shape...  2.07 us

profile of v2, /device:TPU:1, one launch (start us, length us, event | category | flops | bytes accessed | tf_op | source)
XLA Modules:
  0.0 83.9 jit_solution(12212825770032842121)
XLA Ops:
  0.6 8.6 %shard_map.84 = (f32[8,3,8,128]{3,2,1,0:T(8,128)}, f32[8,8,128]{2,1,0:T(8,128)}, s32[8,3,8]{2,1,0:T(4,128)}, s32[8,1,8]{2,1,0:T(1,128)}) custom-call(f32[3,8,128]{2,1,0:T(8,128)} %bitcast.6, f32[8,128]{1,0:T(8,128)} %refs_1_.1, s32[3,8]{1,0:T(4,128)} %bitcast.7, s32[1,8]{1,0:T(1,128)} %bitcast.8), custom_call_target="tpu_custom_call" | custom-call | tf_op jit(solution)/shard_map/pallas_call | solution.py:207
  9.2 2.1 %shard_map.85 = (s32[48]{0:T(128)}, s32[48]{0:T(128)}) custom-call(s32[1]{0:T(128)} %bitcast.3.first_ref, s32[8,3,8]{2,1,0:T(4,128)} %get-tuple-element.18.near_ref, s32[8,1,8]{2,1,0:T(1,128)} %get-tuple-element.19.pos_ref), custom_call_target="tpu_custom_call" | custom-call | tf_op jit(solution)/shard_map/pallas_call | solution.py:254
  11.3 71.1 %shard_map.86 = (f32[8,16,128]{2,1,0:T(8,128)}, f32[3,16]{1,0:T(4,128)}, f32[8,128]{1,0:T(8,128)}, f32[1,8]{1,0:T(1,128)}) custom-call(s32[8,3,8]{2,1,0:T(4,128)} %get-tuple-element.18.near_ref, s32[8,1,8]{2,1,0:T(1,128)} %get-tuple-element.19.pos_ref, s32[48]{0:T(128)} %get-tuple-element.20.slot_ref, s32[48]{0:T(128)} %get-tuple-element.21.local_ref, ...), custom_call_target="tpu_custom_call" | custom-call | tf_op jit(solution)/shard_map/pallas_call | solution.py:569
  82.4 1.5 %shard_map.87 = (f32[8,16,128]{2,1,0:T(8,128)}, f32[3,16]{1,0:T(4,128)}, f32[8,128]{1,0:T(8,128)}, f32[1,8]{1,0:T(1,128)}) custom-call(f32[8,16,128]{2,1,0:T(8,128)} %get-tuple-element.24.refs_0_, f32[3,16]{1,0:T(4,128)} %get-tuple-element.25.refs_1_, f32[8,128]{1,0:T(8,128)} %get-tuple-element.26.refs_2_, f32[1,8]{1,0:T(1,128)} %get-tuple-element.27.refs_3_), custom_call_target="tpu_custom_call" | custom-call | tf_op jit(solution)/shard_map/pallas_call | solution.py:611
